TPU v7x, 32 devices: a whole 2x2x4 slice. The times are simulated.
32 devices in a mesh: day: 2 (over x), row: 16 (over z, y, core).
Axes of the slice: x: 2, y: 2, z: 4, core: 2. Of those that a mesh axis runs over, the one named last changes fastest.
Arguments:
- spectra: bfloat16 [4096, 2, 2, 4096], P(('day', 'row')), parts along dimension 0, may hold values from -110 to 110
- pair_channels: int32 [64, 128, 2], P('row'), may hold values from 0 to 2047, as said below
- pair_live: int32 [64, 128], P('row'), may hold values from 0 to 1, as said below
Outputs:
- correlations: float32 [128, 128, 512], P(('day', 'row')), parts along dimension 0
There are 2 independent parts, one for each index of `day`. A program takes and returns all parts, laid end to end along the dimension named above; an argument that names none is the same for every part. Nothing has to cross between parts.
Inputs may be any that keep to these rules, and one draw needn't show every extreme that they name: `pair_channels`: pair slots of device i of row are tiles i * 4 to (i + 1) * 4 - 1; their first channels are that device's own channels i * 128 to (i + 1) * 128 - 1, and their second channels lie within 128 channels of the first; distances of exactly 128 occur on both sides. `pair_live`: in each device's pair slots (tile by tile, pair by pair) the live slots come first and the padding after; every device has 128 live slots or more, and one device's slots are all live.
All inputs are finite; a program needn't handle non-finite values.
Results may differ from a plain program's by a relative error of at most 0.003.
Values may be sent and summed in bfloat16 or wider, within the bound.
A program may use at most 192 MiB of HBM per device.

v0:
```python
import functools
import math

import jax
import jax.numpy as jnp
from jax import lax
from jax.experimental import pallas as pl
from jax.experimental.pallas import tpu as pltpu
from jax.sharding import PartitionSpec as P

BAND = 64
LAGS = 512
CHUNK = 256
TILE = 512


MESH = pl.DeviceIdType.MESH


def kernel(count, windows, norm_factor, own_hbm, pack_ref, out_ref, own, halo, pack, pick_a, pick_b, white,
           base, acc, back_out, back_in, sums, heard,
           load_sem, send_sem, recv_sem, sum_send, sum_recv, pack_send, pack_recv, back_send, back_recv):
    parts = 2 * windows
    steps, rows, width = own.shape
    half = steps // 2
    chunk = width // parts
    bins = steps * chunk
    pairs = out_ref.shape[0]
    me = lax.axis_index("row")
    first_own = me * rows
    rounds = count.bit_length() - 1
    channels = count * rows
    has_left, has_right = me > 0, me < count - 1

    def load(c, k):
        return pltpu.make_async_copy(
            own_hbm.at[:, pl.ds(pl.multiple_of(k * bins + c * chunk, chunk), chunk)],
            own.at[c, :, pl.ds(k * chunk, chunk)], load_sem.at[c, k])

    def remote(src, dst, sent, got, target):
        return pltpu.make_async_remote_copy(
            src_ref=src, dst_ref=dst, send_sem=sent, recv_sem=got,
            device_id={"row": target}, device_id_type=MESH)

    def send(c, target):
        return remote(own.at[c], halo.at[c], send_sem.at[c], recv_sem.at[c], target)

    def send_pack(side, target):
        return remote(pack_ref, pack.at[side], pack_send.at[side], pack_recv.at[side], target)

    def send_back(side, target):
        return remote(back_out.at[side], back_in.at[side], back_send.at[side], back_recv.at[side], target)

    for k in range(parts):
        @pl.loop(0, steps)
        def _(c, k=k):
            load(c, k).start()

    barrier = pltpu.get_barrier_semaphore()
    partners = [me ^ (1 << r) for r in range(rounds)]
    for partner in partners:
        pl.semaphore_signal(barrier, inc=1, device_id={"row": partner}, device_id_type=MESH)
    other = lax.rem(me + 2 * lax.rem(me, 2) - 1 + count, count)
    pl.semaphore_signal(barrier, inc=1, device_id={"row": other}, device_id_type=MESH)

    acc[...] = jnp.zeros_like(acc)

    @pl.when(jnp.logical_not(has_left))
    def _():
        pack[0] = jnp.zeros(pack.shape[1:], jnp.int32)

        @pl.loop(0, half)
        def _(c):
            halo[c] = jnp.zeros((rows, width), jnp.bfloat16)

    @pl.when(jnp.logical_not(has_right))
    def _():
        pack[1] = jnp.zeros(pack.shape[1:], jnp.int32)

        @pl.loop(half, steps)
        def _(c):
            halo[c] = jnp.zeros((rows, width), jnp.bfloat16)

    @pl.loop(0, steps)
    def _(c):
        for k in range(parts):
            load(c, k).wait()
            block = own[c, :, k * chunk : (k + 1) * chunk].astype(jnp.float32)
            sums[0, c, k : k + 1, :] = jnp.sum(block, axis=0, keepdims=True)

    pl.semaphore_wait(barrier, rounds + 1)

    def add_up(r):
        copy = remote(sums.at[r], heard.at[r], sum_send.at[r], sum_recv.at[r], partners[r])
        copy.start()
        return copy

    copies = [add_up(0)]

    @pl.when(has_right)
    def _():
        send_pack(0, me + 1).start()

    @pl.when(has_left)
    def _():
        send_pack(1, me - 1).start()

    for r in range(rounds):
        if r == 0:
            shifts = lax.broadcasted_iota(jnp.int32, (chunk, LAGS), 1) + (2 * bins - LAGS // 2)
            phase = lax.rem(lax.broadcasted_iota(jnp.int32, (chunk, LAGS), 0) * shifts, 2 * bins)
            angle = phase.astype(jnp.float32) * (math.pi / bins)
            base[0] = jnp.cos(angle)
            base[1] = jnp.sin(angle)
        if r == 1:
            @pl.when(has_left)
            def _():
                send_pack(0, me - 1).wait_recv()

            @pl.when(has_right)
            def _():
                send_pack(1, me + 1).wait_recv()

            row = lax.broadcasted_iota(jnp.int32, (2 * rows, pairs), 0)
            for side in range(2):
                beside = first_own - rows if side == 0 else first_own + rows

                def pick(index, near):
                    inside = (index >= first_own) & (index < first_own + rows)
                    mine = jnp.where(inside, index - first_own + rows, -1)
                    if not near:
                        return mine
                    across = (index >= beside) & (index < beside + rows)
                    return jnp.where(across, index - beside, mine)

                for group in range(2):
                    table = pack_ref[...] if group == side_own(side) else pack[side]
                    first, second, live = table[0:1], table[1:2], table[2:3].astype(jnp.float32)
                    near = group == side_own(side)
                    at = slice(group * pairs, (group + 1) * pairs)
                    a_row = pick(first, True)
                    b_row = pick(second, near)
                    hot_a = (row == a_row).astype(jnp.float32) * live
                    hot_b = (row == b_row).astype(jnp.float32)
                    pick_a[side, at, :] = jnp.transpose(hot_a).astype(jnp.bfloat16)
                    pick_b[side, at, :] = jnp.transpose(hot_b).astype(jnp.bfloat16)
        copies[r].wait_recv()
        sums[r + 1] = sums[r] + heard[r]
        if r + 1 < rounds:
            copies.append(add_up(r + 1))

    @pl.when(has_right)
    def _():
        @pl.loop(0, half)
        def _(c):
            send(c, me + 1).start()

    lane_r = lax.broadcasted_iota(jnp.int32, (chunk, chunk), 0) // BAND
    lane_c = lax.broadcasted_iota(jnp.int32, (chunk, chunk), 1) // BAND
    same = (lane_r == lane_c).astype(jnp.float32).astype(jnp.bfloat16)

    def whiten(c, source, start):
        common = sums[rounds, c] * (1.0 / channels)
        for w in range(windows):
            at = 2 * w * chunk
            re = source[:, at : at + chunk].astype(jnp.float32) - common[2 * w : 2 * w + 1, :]
            im = source[:, at + chunk : at + 2 * chunk].astype(jnp.float32) - common[2 * w + 1 : 2 * w + 2, :]
            power = re * re + im * im
            mag = power * lax.rsqrt(jnp.maximum(power, 1e-30))
            hi = mag.astype(jnp.bfloat16)
            lo = (mag - hi.astype(jnp.float32)).astype(jnp.bfloat16)
            level = jnp.dot(hi, same, preferred_element_type=jnp.float32)
            level += jnp.dot(lo, same, preferred_element_type=jnp.float32)
            scale = 1.0 / (level * (1.0 / BAND) + 1e-06)
            white[start : start + rows, at : at + chunk] = (re * scale).astype(jnp.bfloat16)
            white[start : start + rows, at + chunk : at + 2 * chunk] = (im * scale).astype(jnp.bfloat16)

    shift_row = lax.broadcasted_iota(jnp.int32, (8, LAGS), 1) + (2 * bins - LAGS // 2)

    def correlate(side, c):
        turn = lax.rem(lax.rem(c * shift_row, 2 * bins) * chunk, 2 * bins).astype(jnp.float32) * (math.pi / bins)
        ch, sh = jnp.cos(turn)[0:1], jnp.sin(turn)[0:1]
        lag_re = (base[0] * ch - base[1] * sh).astype(jnp.bfloat16)
        lag_im = (-(base[1] * ch + base[0] * sh)).astype(jnp.bfloat16)
        tile = TILE

        @pl.loop(0, 2 * pairs // tile)
        def _(i):
            at = pl.ds(pl.multiple_of(i * tile, tile), tile)
            to = pl.ds(pl.multiple_of(side * pairs + i * tile, tile), tile)
            cross_re = jnp.zeros((tile, chunk), jnp.float32)
            cross_im = jnp.zeros((tile, chunk), jnp.float32)
            for w in range(windows):
                lo = 2 * w * chunk
                a = jnp.dot(pick_a[side, at, :], white[:, lo : lo + 2 * chunk], preferred_element_type=jnp.float32)
                b = jnp.dot(pick_b[side, at, :], white[:, lo : lo + 2 * chunk], preferred_element_type=jnp.float32)
                ar, ai, br, bi = a[:, :chunk], a[:, chunk:], b[:, :chunk], b[:, chunk:]
                cross_re += ar * br + ai * bi
                cross_im += ai * br - ar * bi
            total = jnp.dot(cross_re.astype(jnp.bfloat16), lag_re, preferred_element_type=jnp.float32)
            total += jnp.dot(cross_im.astype(jnp.bfloat16), lag_im, preferred_element_type=jnp.float32)
            acc[to, :] += total

    @pl.loop(0, half)
    def _(c):
        @pl.when(has_left & (c >= half // 2))
        def _():
            send(2 * c, me - 1).start()
            send(2 * c + 1, me - 1).start()

        whiten(c, own.at[c], rows)

        @pl.when(has_left)
        def _():
            send(c, me - 1).wait_recv()

        whiten(c, halo.at[c], 0)
        correlate(0, c)

    back_out[0] = acc[0:pairs, :].astype(jnp.bfloat16)

    @pl.when(has_left)
    def _():
        send_back(0, me - 1).start()

    @pl.loop(half, steps)
    def _(c):
        whiten(c, own.at[c], rows)

        @pl.when(has_right)
        def _():
            send(c, me + 1).wait_recv()

        whiten(c, halo.at[c], 0)
        correlate(1, c)

    back_out[1] = acc[2 * pairs : 3 * pairs, :].astype(jnp.bfloat16)

    @pl.when(has_right)
    def _():
        send_back(1, me + 1).start()
        send_back(0, me + 1).wait_recv()
        acc[pairs : 2 * pairs, :] += back_in[0].astype(jnp.float32)

    @pl.when(has_left)
    def _():
        send_back(1, me - 1).wait_recv()
        acc[pairs : 2 * pairs, :] += back_in[1].astype(jnp.float32)

    out_ref[...] = acc[pairs : 2 * pairs, :] * norm_factor
    for copy in copies:
        copy.wait_send()

    @pl.when(has_right)
    def _():
        send_pack(0, me + 1).wait_send()
        send_back(1, me + 1).wait_send()

        @pl.loop(0, half)
        def _(c):
            send(c, me + 1).wait_send()

    @pl.when(has_left)
    def _():
        send_pack(1, me - 1).wait_send()
        send_back(0, me - 1).wait_send()

        @pl.loop(half, steps)
        def _(c):
            send(c, me - 1).wait_send()


def side_own(side):
    return 1 - side


def body(spectra, pair_channels, pair_live):
    rows, windows, _, bins = spectra.shape
    count = lax.axis_size("row")
    parts = 2 * windows
    flat = spectra.reshape(rows, parts * bins)
    steps = bins // CHUNK
    tile_count, tile_pairs = pair_live.shape
    pairs = tile_count * tile_pairs
    index = jnp.transpose(pair_channels, (2, 0, 1)).reshape(2, pairs)
    packed = jnp.concatenate([index, pair_live.reshape(1, pairs)], axis=0)
    rounds = count.bit_length() - 1
    vmem = pl.BlockSpec(memory_space=pltpu.VMEM)
    dma = pltpu.SemaphoreType.DMA
    result = pl.pallas_call(
        functools.partial(kernel, count, windows, 1.0 / math.sqrt(bins * windows)),
        out_shape=jax.ShapeDtypeStruct((pairs, LAGS), jnp.float32),
        in_specs=[pl.BlockSpec(memory_space=pl.ANY), vmem],
        out_specs=vmem,
        scratch_shapes=[
            pltpu.VMEM((steps, rows, parts * CHUNK), jnp.bfloat16),
            pltpu.VMEM((steps, rows, parts * CHUNK), jnp.bfloat16),
            pltpu.VMEM((2, 3, pairs), jnp.int32),
            pltpu.VMEM((2, 2 * pairs, 2 * rows), jnp.bfloat16),
            pltpu.VMEM((2, 2 * pairs, 2 * rows), jnp.bfloat16),
            pltpu.VMEM((2 * rows, parts * CHUNK), jnp.bfloat16),
            pltpu.VMEM((2, CHUNK, LAGS), jnp.float32),
            pltpu.VMEM((3 * pairs, LAGS), jnp.float32),
            pltpu.VMEM((2, pairs, LAGS), jnp.bfloat16),
            pltpu.VMEM((2, pairs, LAGS), jnp.bfloat16),
            pltpu.VMEM((rounds + 1, steps, parts, CHUNK), jnp.float32),
            pltpu.VMEM((rounds, steps, parts, CHUNK), jnp.float32),
            dma((steps, parts)), dma((steps,)), dma((steps,)), dma((rounds,)), dma((rounds,)),
            dma((2,)), dma((2,)), dma((2,)), dma((2,)),
        ],
        compiler_params=pltpu.CompilerParams(
            collective_id=0, has_side_effects=True, vmem_limit_bytes=60 * 2**20),
    )(flat, packed)
    return result.reshape(tile_count, tile_pairs, LAGS)


def solution(mesh):
    placed = (P(("day", "row"), None, None, None), P("row", None, None), P("row", None))
    return jax.shard_map(
        body, mesh=mesh, in_specs=placed, out_specs=P(("day", "row"), None, None), check_vma=False
    )
```

profile of v0, /device:TPU:7, one launch (start us, length us, event | category | flops | bytes accessed | tf_op | source)
XLA Modules:
  0.0 111.3 jit_solution(4548321279220527280)
XLA Ops:
  0.0 1.3 %pad_add_fusion.pack_ref = s32[3,512]{1,0:T(4,128)} fusion(s32[1,512]{1,0:T(1,128)} %bitcast.7, s32[2,512]{1,0:T(2,128)} %bitcast.6), kind=kLoop, calls=%fused_computation | loop fusion | flops 1536 | bytes 12288 | tf_op jit(solution)/shard_map/concatenate | solution.py:286
  1.3 7.8 %reshape.12.own_hbm = bf16[128,16384]{1,0:T(8,128)(2,1)} reshape(bf16[128,2,2,4096]{3,2,1,0:T(2,128)(2,1)} %param.3) | data formatting | bytes 8388608 | tf_op jit(solution)/shard_map/reshape | solution.py:281
  9.1 99.9 %shard_map.37 = f32[512,512]{1,0:T(8,128)} custom-call(bf16[128,16384]{1,0:T(8,128)(2,1)} %reshape.12.own_hbm, s32[3,512]{1,0:T(4,128)} %pad_add_fusion.pack_ref), custom_call_target="tpu_custom_call" | custom-call | tf_op jit(solution)/shard_map/pallas_call | solution.py:290
  109.0 2.3 %copy.5 = f32[4,128,512]{2,1,0:T(8,128)} copy(f32[4,128,512]{2,1,0:T(8,128)} %bitcast.5) | data formatting | bytes 2097152
where the time goes:
time: 112 us; the launch traced here: 111 us
  Pallas kernels  99.9 us (89%)
  local copies, waits for them, and re-layouts  10.1 us (9%)
  other arithmetic  1.31 us (1%)
    pallas_call x1, Pallas kernels, body(): pl.pallas_call(functools.partial(kernel, count, windows, 1.0 / math.sqrt(...  99.9 us
    reshape x1, local copies, waits for them, and re-layouts, body(): flat = spectra.reshape(rows, parts * bins)  7.82 us
    unnamed x1, local copies, waits for them, and re-layouts  2.26 us

commit v1 on v0

v1 whole, which is shorter than its diff:
```python
import functools
import math

import jax
import jax.numpy as jnp
from jax import lax
from jax.experimental import pallas as pl
from jax.experimental.pallas import tpu as pltpu
from jax.sharding import PartitionSpec as P

BAND = 64
LAGS = 512
LANES = 128
SLAB = 8 * LANES
PIECES = 4
WHITEN_ROWS = 64
UNROLL = 16
EARLY = 2
MESH = pl.DeviceIdType.MESH


def kernel(count, windows, norm_factor, own_hbm, pairs_ref, live_ref, out_ref,
           own, beside, across, white, spread, planes, lag, acc, base, turn,
           sums, heard_half, red, heard, other_half, common,
           far_pairs, far_live, tab_v, tab_a0, tab_b0, tab_a1, tab_b1, back_out, back_in,
           load_sem, beside_send, beside_recv, across_send, across_recv, sum_send, sum_recv,
           tab_send, tab_recv, back_send, back_recv, smem_sem):
    slabs, rows = own.shape[:2]
    half = slabs // 2
    span = windows * 16
    bins = slabs * SLAB
    pairs = out_ref.shape[0]
    me = lax.axis_index("row")
    core = lax.rem(me, 2)
    partner = me + 1 - 2 * core
    rounds = count.bit_length() - 1
    channels = count * rows
    piece = rows // PIECES
    gets = (core == 1) & (me < count - 1)
    gives = (core == 0) & (me > 0)
    right, left = lax.rem(me + 1, count), lax.rem(me + count - 1, count)
    near = jnp.where(core == 1, right, left)
    zero_row = 3 * rows

    def remote(src, dst, sent, got, target):
        return pltpu.make_async_remote_copy(
            src_ref=src, dst_ref=dst, send_sem=sent, recv_sem=got,
            device_id={"row": target}, device_id_type=MESH)

    def load(q):
        return pltpu.make_async_copy(own_hbm.at[:, :, q], own.at[q], load_sem.at[q])

    def send_beside(q):
        return remote(own_hbm.at[:, :, q], beside.at[q], beside_send.at[q], beside_recv.at[q], partner)

    def send_across(q, k, target):
        at = pl.ds(pl.multiple_of(k * piece, piece), piece)
        return remote(own_hbm.at[at, :, q], across.at[q, at], across_send.at[q, k], across_recv.at[q, k], target)

    def send_tables(target):
        return (remote(pairs_ref, far_pairs, tab_send.at[0], tab_recv.at[0], target),
                remote(live_ref, far_live, tab_send.at[1], tab_recv.at[1], target))

    def send_back(target):
        return remote(back_out, back_in, back_send.at[0], back_recv.at[0], target)

    for q in range(slabs):
        load(q).start()

    barrier = pltpu.get_barrier_semaphore()
    partners = [me ^ (1 << r) for r in range(rounds)]
    for p in partners:
        pl.semaphore_signal(barrier, inc=1, device_id={"row": p}, device_id_type=MESH)

    pl.semaphore_signal(barrier, inc=1, device_id={"row": near}, device_id_type=MESH)
    pl.semaphore_wait(barrier, rounds + 1)

    @pl.when(gives)
    def _():
        for copy in send_tables(left):
            copy.start()
        for k in range(EARLY):
            send_across(0, k, left).start()

    for q in range(slabs):
        send_beside(q).start()

    acc[...] = jnp.zeros_like(acc)
    white[pl.ds(zero_row, 8)] = jnp.zeros((8,) + white.shape[1:], jnp.float32)

    for q in range(slabs):
        load(q).wait()

        def step(i, total):
            block = own[q, pl.ds(pl.multiple_of(i * 8, 8), 8)].astype(jnp.float32)
            return total + jnp.sum(block, axis=0)

        total = lax.fori_loop(0, rows // 8, step, jnp.zeros((windows, 16, LANES), jnp.float32))
        sums[q // half, pl.ds((q % half) * span, span), :] = total.reshape(span, LANES)

    copies = []

    def exchange(r, src, dst):
        copy = remote(src, dst, sum_send.at[r], sum_recv.at[r], partners[r] if r < rounds else partner)
        copy.start()
        copies.append(copy)

    exchange(0, sums.at[1 - core], heard_half)
    shifts = lax.broadcasted_iota(jnp.int32, (LANES, LAGS), 1) + (2 * bins - LAGS // 2)
    phase = lax.rem(lax.broadcasted_iota(jnp.int32, (LANES, LAGS), 0) * shifts, 2 * bins)
    angle = phase.astype(jnp.float32) * (math.pi / bins)
    base[0] = jnp.cos(angle)
    base[1] = jnp.sin(angle)
    copies[0].wait_recv()
    red[0] = sums[core] + heard_half[...]

    tiles = bins // LANES
    for r in range(1, rounds):
        exchange(r, red.at[r - 1], heard.at[r - 1])
        if r == 1:
            @pl.when(gives)
            def _():
                for k in range(EARLY, PIECES):
                    send_across(0, k, left).start()

                @pl.loop(1, slabs)
                def _(q):
                    for k in range(PIECES):
                        send_across(q, k, left).start()

            shift_row = lax.broadcasted_iota(jnp.int32, (tiles, LAGS), 1) + (2 * bins - LAGS // 2)
            turns = lax.rem(lax.broadcasted_iota(jnp.int32, (tiles, LAGS), 0) * shift_row, 2 * bins)
            turned = lax.rem(turns * LANES, 2 * bins).astype(jnp.float32) * (math.pi / bins)
            turn[0] = jnp.cos(turned)
            turn[1] = jnp.sin(turned)

        @pl.loop((r - 1) * slabs // (rounds - 1), r * slabs // (rounds - 1))
        def _(q):
            @pl.loop(0, 8)
            def _(f):
                ch = turn[0, pl.ds(q * 8 + f, 1), :]
                sh = turn[1, pl.ds(q * 8 + f, 1), :]

                @pl.loop(0, LANES // 16)
                def _(k):
                    at = pl.ds(pl.multiple_of(k * 16, 16), 16)
                    to = pl.ds(pl.multiple_of(f * LANES + k * 16, 16), 16)
                    bc, bs = base[0, at, :], base[1, at, :]
                    lag[q, 0, to, :] = (bc * ch - bs * sh).astype(jnp.bfloat16)
                    lag[q, 1, to, :] = (-(bs * ch + bc * sh)).astype(jnp.bfloat16)

        copies[r].wait_recv()
        red[r] = red[r - 1] + heard[r - 1]
    exchange(rounds, red.at[rounds - 1], other_half)

    def place(index, regions):
        slot = jnp.full_like(index, zero_row)
        for device, start in regions:
            offset = index - device * rows
            slot = jnp.where((offset >= 0) & (offset < rows), offset + start, slot)
        return slot

    first, second, live = pairs_ref[0:1], pairs_ref[1:2], live_ref[...]
    far_device = jnp.where(gets, me + 1, -2)
    regions = ((me, 0), (partner, rows), (far_device, 2 * rows))
    tab_v[0] = jnp.where(live > 0, place(first, regions), zero_row)
    tab_v[1] = place(second, regions)

    @pl.when(gets)
    def _():
        for copy in send_tables(right):
            copy.wait_recv()
        tab_v[2] = jnp.where(far_live[...] > 0, place(far_pairs[0:1], ((me + 1, 2 * rows),)), zero_row)
        tab_v[3] = place(far_pairs[1:2], ((me, 0),))

    @pl.when(jnp.logical_not(gets))
    def _():
        tab_v[2] = jnp.full((1, pairs), zero_row, jnp.int32)
        tab_v[3] = jnp.full((1, pairs), zero_row, jnp.int32)

    tables = (tab_a0, tab_b0, tab_a1, tab_b1)
    moves = [pltpu.make_async_copy(tab_v.at[i], table, smem_sem.at[i]) for i, table in enumerate(tables)]
    for move in moves:
        move.start()

    copies[rounds].wait_recv()
    per = half * windows * 8
    for r in range(2):
        common[r, pl.ds(core * half, half)] = (
            red[rounds - 1, pl.ds(r, per, stride=2), :] * (1.0 / channels)).reshape(half, windows * 8, LANES)
        common[r, pl.ds((1 - core) * half, half)] = (
            other_half[pl.ds(r, per, stride=2), :] * (1.0 / channels)).reshape(half, windows * 8, LANES)
    for move in moves:
        move.wait()

    lane_r = lax.broadcasted_iota(jnp.int32, (LANES, LANES), 0) // BAND
    lane_c = lax.broadcasted_iota(jnp.int32, (LANES, LANES), 1) // BAND
    same = (lane_r == lane_c).astype(jnp.float32).astype(jnp.bfloat16)
    size = WHITEN_ROWS
    depth = windows * 8

    def whiten(q, source, i, start):
        at = pl.ds(pl.multiple_of(i * size, size), size)
        spread[...] = source[q, at].astype(jnp.float32).reshape(size * span, LANES)
        re = spread[pl.ds(0, size * depth, stride=2), :].reshape(size, depth, LANES) - common[0, q][None]
        im = spread[pl.ds(1, size * depth, stride=2), :].reshape(size, depth, LANES) - common[1, q][None]
        power = (re * re + im * im).reshape(size * depth, LANES)
        mag = power * lax.rsqrt(jnp.maximum(power, 1e-30))
        hi = mag.astype(jnp.bfloat16)
        lo = (mag - hi.astype(jnp.float32)).astype(jnp.bfloat16)
        level = jnp.dot(hi, same, preferred_element_type=jnp.float32)
        level += jnp.dot(lo, same, preferred_element_type=jnp.float32)
        scale = (1.0 / (level * (1.0 / BAND) + 1e-06)).reshape(size, depth, LANES)
        to = pl.ds(pl.multiple_of(start + i * size, 8), size)
        wr = (re * scale).astype(jnp.bfloat16).astype(jnp.float32)
        wi = (im * scale).astype(jnp.bfloat16).astype(jnp.float32)
        white[to, 0:windows] = wr.reshape(size, windows, 8, LANES)
        white[to, windows : 2 * windows] = wi.reshape(size, windows, 8, LANES)

    def whiten_all(q, source, start):
        @pl.loop(0, rows // size)
        def _(i):
            whiten(q, source, i, start)

    def correlate(group, q):
        table_a, table_b = tables[2 * group], tables[2 * group + 1]

        @pl.loop(0, pairs // UNROLL)
        def _(i):
            at = pl.multiple_of(i * UNROLL * 8, 64)
            for u in range(UNROLL):
                p = i * UNROLL + u
                a, b = white.at[table_a[0, p]], white.at[table_b[0, p]]
                cross_re, cross_im = None, None
                for w in range(windows):
                    ar, ai, br, bi = a[w], a[windows + w], b[w], b[windows + w]
                    part_re, part_im = ar * br + ai * bi, ai * br - ar * bi
                    cross_re = part_re if cross_re is None else cross_re + part_re
                    cross_im = part_im if cross_im is None else cross_im + part_im
                to = pl.ds(at + (u // 8) * 64 + u % 8, 8, stride=8)
                planes[0, to, :] = cross_re
                planes[1, to, :] = cross_im

        total = None
        for r in range(2):
            plane = planes[r].reshape(pairs // 8, 8, 8, LANES)
            cross = jnp.concatenate([plane[:, f].reshape(pairs, LANES).astype(jnp.bfloat16) for f in range(8)], axis=1)
            part = jnp.dot(cross, lag[q, r], preferred_element_type=jnp.float32)
            total = part if total is None else total + part
        acc[group] += total

    @pl.loop(0, slabs)
    def _(q):
        whiten_all(q, own, 0)
        send_beside(q).wait_recv()
        whiten_all(q, beside, rows)

        @pl.when(gets)
        def _():
            for k in range(PIECES):
                send_across(q, k, right).wait_recv()
            whiten_all(q, across, 2 * rows)
            correlate(1, q)

            @pl.when(q == slabs - 1)
            def _():
                back_out[...] = acc[1].astype(jnp.bfloat16)
                send_back(right).start()

        correlate(0, q)

    @pl.when(gives)
    def _():
        send_back(left).wait_recv()
        acc[0] += back_in[...].astype(jnp.float32)

    out_ref[...] = acc[0] * norm_factor

    for copy in copies:
        copy.wait_send()
    for q in range(slabs):
        send_beside(q).wait_send()

    @pl.when(gives)
    def _():
        for copy in send_tables(left):
            copy.wait_send()

        @pl.loop(0, slabs)
        def _(q):
            for k in range(PIECES):
                send_across(q, k, left).wait_send()

    @pl.when(gets)
    def _():
        send_back(right).wait_send()


def body(spectra, pair_channels, pair_live):
    rows, windows, _, bins = spectra.shape
    count = lax.axis_size("row")
    slabs = bins // SLAB
    view = spectra.reshape(rows, windows, 2, bins // LANES, LANES).transpose(0, 1, 3, 2, 4)
    view = view.reshape(rows, windows, slabs, 16, LANES)
    tile_count, tile_pairs = pair_live.shape
    pairs = tile_count * tile_pairs
    index = jnp.transpose(pair_channels, (2, 0, 1)).reshape(2, pairs)
    live = pair_live.reshape(1, pairs)
    rounds = count.bit_length() - 1
    half = slabs // 2
    span = windows * 16
    vmem = pl.BlockSpec(memory_space=pltpu.VMEM)
    dma = pltpu.SemaphoreType.DMA
    f32, bf16, i32 = jnp.float32, jnp.bfloat16, jnp.int32
    raw = pltpu.VMEM((slabs, rows, windows, 16, LANES), bf16)
    result = pl.pallas_call(
        functools.partial(kernel, count, windows, 1.0 / math.sqrt(bins * windows)),
        out_shape=jax.ShapeDtypeStruct((pairs, LAGS), f32),
        in_specs=[pl.BlockSpec(memory_space=pl.ANY), vmem, vmem],
        out_specs=vmem,
        scratch_shapes=[
            raw, raw, raw,
            pltpu.VMEM((3 * rows + 8, 2 * windows, 8, LANES), f32),
            pltpu.VMEM((WHITEN_ROWS * span, LANES), f32),
            pltpu.VMEM((2, pairs * 8, LANES), f32),
            pltpu.VMEM((slabs, 2, SLAB, LAGS), bf16),
            pltpu.VMEM((2, pairs, LAGS), f32),
            pltpu.VMEM((2, LANES, LAGS), f32),
            pltpu.VMEM((2, bins // LANES, LAGS), f32),
            pltpu.VMEM((2, half * span, LANES), f32),
            pltpu.VMEM((half * span, LANES), f32),
            pltpu.VMEM((rounds, half * span, LANES), f32),
            pltpu.VMEM((rounds - 1, half * span, LANES), f32),
            pltpu.VMEM((half * span, LANES), f32),
            pltpu.VMEM((2, slabs, windows * 8, LANES), f32),
            pltpu.VMEM((2, pairs), i32),
            pltpu.VMEM((1, pairs), i32),
            pltpu.VMEM((4, 1, pairs), i32),
            pltpu.SMEM((1, pairs), i32), pltpu.SMEM((1, pairs), i32),
            pltpu.SMEM((1, pairs), i32), pltpu.SMEM((1, pairs), i32),
            pltpu.VMEM((pairs, LAGS), bf16),
            pltpu.VMEM((pairs, LAGS), bf16),
            dma((slabs,)), dma((slabs,)), dma((slabs,)), dma((slabs, PIECES)), dma((slabs, PIECES)),
            dma((rounds + 1,)), dma((rounds + 1,)), dma((2,)), dma((2,)), dma((1,)), dma((1,)), dma((4,)),
        ],
        compiler_params=pltpu.CompilerParams(
            collective_id=0, has_side_effects=True, vmem_limit_bytes=60 * 2**20),
    )(view, index, live)
    return result.reshape(tile_count, tile_pairs, LAGS)


def solution(mesh):
    placed = (P(("day", "row"), None, None, None), P("row", None, None), P("row", None))
    return jax.shard_map(
        body, mesh=mesh, in_specs=placed, out_specs=P(("day", "row"), None, None), check_vma=False
    )
```

time: 112 us -> 100 us (0.89)
  the two profiles are of different devices: /device:TPU:7 before, /device:TPU:6 now
where the time goes in v1:
time: 100 us; the launch traced here: 99.8 us
  Pallas kernels  97.6 us (98%)
  local copies, waits for them, and re-layouts  2.26 us (2%)
    pallas_call x1, Pallas kernels, body(): pl.pallas_call(functools.partial(kernel, count, windows, 1.0 / math.sqrt(...  97.6 us
    unnamed x1, local copies, waits for them, and re-layouts  2.26 us

profile of v1, /device:TPU:6, one launch (start us, length us, event | category | flops | bytes accessed | tf_op | source)
XLA Modules:
  0.0 99.8 jit_solution(227630943768909972)
XLA Ops:
  0.0 97.6 %shard_map.37 = f32[512,512]{1,0:T(8,128)} custom-call(bf16[128,2,4,16,128]{4,3,2,1,0:T(8,128)(2,1)} %bitcast.10, s32[2,512]{1,0:T(2,128)} %bitcast.12, s32[1,512]{1,0:T(1,128)} %bitcast.13), custom_call_target="tpu_custom_call" | custom-call | tf_op jit(solution)/shard_map/pallas_call | solution.py:316
  97.6 2.3 %copy.6 = f32[4,128,512]{2,1,0:T(8,128)} copy(f32[4,128,512]{2,1,0:T(8,128)} %bitcast.11) | data formatting | bytes 2097152

commit v2 on v1

--- a/solution.py
+++ b/solution.py
@@ -15,18 +15,16 @@
 PIECES = 4
 WHITEN_ROWS = 64
 UNROLL = 16
-EARLY = 2
 MESH = pl.DeviceIdType.MESH
 
 
 def kernel(count, windows, norm_factor, own_hbm, pairs_ref, live_ref, out_ref,
            own, beside, across, white, spread, planes, lag, acc, base, turn,
-           sums, heard_half, red, heard, other_half, common,
+           sums, handed, red, heard, common,
            far_pairs, far_live, tab_v, tab_a0, tab_b0, tab_a1, tab_b1, back_out, back_in,
            load_sem, beside_send, beside_recv, across_send, across_recv, sum_send, sum_recv,
            tab_send, tab_recv, back_send, back_recv, smem_sem):
     slabs, rows = own.shape[:2]
-    half = slabs // 2
     span = windows * 16
     bins = slabs * SLAB
     pairs = out_ref.shape[0]
@@ -68,19 +66,26 @@
         load(q).start()
 
     barrier = pltpu.get_barrier_semaphore()
-    partners = [me ^ (1 << r) for r in range(rounds)]
-    for p in partners:
+    hops = [me ^ (1 << r) for r in range(1, rounds)]
+    for p in (partner, near):
         pl.semaphore_signal(barrier, inc=1, device_id={"row": p}, device_id_type=MESH)
 
-    pl.semaphore_signal(barrier, inc=1, device_id={"row": near}, device_id_type=MESH)
-    pl.semaphore_wait(barrier, rounds + 1)
+    @pl.when(core == 1)
+    def _():
+        for p in hops:
+            pl.semaphore_signal(barrier, inc=1, device_id={"row": p}, device_id_type=MESH)
+
+    pl.semaphore_wait(barrier, 2 + core * len(hops))
 
     @pl.when(gives)
     def _():
         for copy in send_tables(left):
             copy.start()
-        for k in range(EARLY):
-            send_across(0, k, left).start()
+
+        @pl.loop(0, slabs)
+        def _(q):
+            for k in range(PIECES):
+                send_across(q, k, left).start()
 
     for q in range(slabs):
         send_beside(q).start()
@@ -96,45 +101,42 @@
             return total + jnp.sum(block, axis=0)
 
         total = lax.fori_loop(0, rows // 8, step, jnp.zeros((windows, 16, LANES), jnp.float32))
-        sums[q // half, pl.ds((q % half) * span, span), :] = total.reshape(span, LANES)
-
-    copies = []
-
-    def exchange(r, src, dst):
-        copy = remote(src, dst, sum_send.at[r], sum_recv.at[r], partners[r] if r < rounds else partner)
-        copy.start()
-        copies.append(copy)
-
-    exchange(0, sums.at[1 - core], heard_half)
+        sums[pl.ds(q * span, span), :] = total.reshape(span, LANES)
+
+    def hand_over():
+        return remote(sums, handed, sum_send.at[0], sum_recv.at[0], partner)
+
+    def hop(r):
+        return remote(red.at[r], heard.at[r], sum_send.at[r + 1], sum_recv.at[r + 1], hops[r])
+
+    def hand_back():
+        return remote(red.at[rounds - 1], handed, sum_send.at[rounds], sum_recv.at[rounds], partner)
+
+    @pl.when(core == 0)
+    def _():
+        hand_over().start()
+
     shifts = lax.broadcasted_iota(jnp.int32, (LANES, LAGS), 1) + (2 * bins - LAGS // 2)
     phase = lax.rem(lax.broadcasted_iota(jnp.int32, (LANES, LAGS), 0) * shifts, 2 * bins)
     angle = phase.astype(jnp.float32) * (math.pi / bins)
     base[0] = jnp.cos(angle)
     base[1] = jnp.sin(angle)
-    copies[0].wait_recv()
-    red[0] = sums[core] + heard_half[...]
+
+    @pl.when(core == 1)
+    def _():
+        hand_over().wait_recv()
+        red[0] = sums[...] + handed[...]
+        hop(0).start()
 
     tiles = bins // LANES
-    for r in range(1, rounds):
-        exchange(r, red.at[r - 1], heard.at[r - 1])
-        if r == 1:
-            @pl.when(gives)
-            def _():
-                for k in range(EARLY, PIECES):
-                    send_across(0, k, left).start()
-
-                @pl.loop(1, slabs)
-                def _(q):
-                    for k in range(PIECES):
-                        send_across(q, k, left).start()
-
-            shift_row = lax.broadcasted_iota(jnp.int32, (tiles, LAGS), 1) + (2 * bins - LAGS // 2)
-            turns = lax.rem(lax.broadcasted_iota(jnp.int32, (tiles, LAGS), 0) * shift_row, 2 * bins)
-            turned = lax.rem(turns * LANES, 2 * bins).astype(jnp.float32) * (math.pi / bins)
-            turn[0] = jnp.cos(turned)
-            turn[1] = jnp.sin(turned)
-
-        @pl.loop((r - 1) * slabs // (rounds - 1), r * slabs // (rounds - 1))
+    shift_row = lax.broadcasted_iota(jnp.int32, (tiles, LAGS), 1) + (2 * bins - LAGS // 2)
+    turns = lax.rem(lax.broadcasted_iota(jnp.int32, (tiles, LAGS), 0) * shift_row, 2 * bins)
+    turned = lax.rem(turns * LANES, 2 * bins).astype(jnp.float32) * (math.pi / bins)
+    turn[0] = jnp.cos(turned)
+    turn[1] = jnp.sin(turned)
+
+    for r in range(rounds - 1):
+        @pl.loop(r * slabs // (rounds - 1), (r + 1) * slabs // (rounds - 1))
         def _(q):
             @pl.loop(0, 8)
             def _(f):
@@ -149,9 +151,14 @@
                     lag[q, 0, to, :] = (bc * ch - bs * sh).astype(jnp.bfloat16)
                     lag[q, 1, to, :] = (-(bs * ch + bc * sh)).astype(jnp.bfloat16)
 
-        copies[r].wait_recv()
-        red[r] = red[r - 1] + heard[r - 1]
-    exchange(rounds, red.at[rounds - 1], other_half)
+        @pl.when(core == 1)
+        def _():
+            hop(r).wait_recv()
+            red[r + 1] = red[r] + heard[r]
+            if r + 2 < rounds:
+                hop(r + 1).start()
+            else:
+                hand_back().start()
 
     def place(index, regions):
         slot = jnp.full_like(index, zero_row)
@@ -183,13 +190,20 @@
     for move in moves:
         move.start()
 
-    copies[rounds].wait_recv()
-    per = half * windows * 8
-    for r in range(2):
-        common[r, pl.ds(core * half, half)] = (
-            red[rounds - 1, pl.ds(r, per, stride=2), :] * (1.0 / channels)).reshape(half, windows * 8, LANES)
-        common[r, pl.ds((1 - core) * half, half)] = (
-            other_half[pl.ds(r, per, stride=2), :] * (1.0 / channels)).reshape(half, windows * 8, LANES)
+    def set_common(total):
+        for r in range(2):
+            strided = total[pl.ds(r, slabs * windows * 8, stride=2), :] * (1.0 / channels)
+            common[r] = strided.reshape(slabs, windows * 8, LANES)
+
+    @pl.when(core == 1)
+    def _():
+        set_common(red.at[rounds - 1])
+
+    @pl.when(core == 0)
+    def _():
+        hand_back().wait_recv()
+        set_common(handed)
+
     for move in moves:
         move.wait()
 
@@ -276,10 +290,18 @@
 
     out_ref[...] = acc[0] * norm_factor
 
-    for copy in copies:
-        copy.wait_send()
     for q in range(slabs):
         send_beside(q).wait_send()
+
+    @pl.when(core == 0)
+    def _():
+        hand_over().wait_send()
+
+    @pl.when(core == 1)
+    def _():
+        for r in range(rounds - 1):
+            hop(r).wait_send()
+        hand_back().wait_send()
 
     @pl.when(gives)
     def _():
@@ -307,7 +329,6 @@
     index = jnp.transpose(pair_channels, (2, 0, 1)).reshape(2, pairs)
     live = pair_live.reshape(1, pairs)
     rounds = count.bit_length() - 1
-    half = slabs // 2
     span = windows * 16
     vmem = pl.BlockSpec(memory_space=pltpu.VMEM)
     dma = pltpu.SemaphoreType.DMA
@@ -327,11 +348,10 @@
             pltpu.VMEM((2, pairs, LAGS), f32),
             pltpu.VMEM((2, LANES, LAGS), f32),
             pltpu.VMEM((2, bins // LANES, LAGS), f32),
-            pltpu.VMEM((2, half * span, LANES), f32),
-            pltpu.VMEM((half * span, LANES), f32),
-            pltpu.VMEM((rounds, half * span, LANES), f32),
-            pltpu.VMEM((rounds - 1, half * span, LANES), f32),
-            pltpu.VMEM((half * span, LANES), f32),
+            pltpu.VMEM((slabs * span, LANES), f32),
+            pltpu.VMEM((slabs * span, LANES), f32),
+            pltpu.VMEM((rounds, slabs * span, LANES), f32),
+            pltpu.VMEM((rounds - 1, slabs * span, LANES), f32),
             pltpu.VMEM((2, slabs, windows * 8, LANES), f32),
             pltpu.VMEM((2, pairs), i32),
             pltpu.VMEM((1, pairs), i32),

time: 100 us -> 66.8 us (0.67)
  the two profiles are of different devices: /device:TPU:6 before, /device:TPU:16 now
where the time goes in v2:
time: 66.8 us; the launch traced here: 66.7 us
  Pallas kernels  64.4 us (96%)
  local copies, waits for them, and re-layouts  2.26 us (3%)
    pallas_call x1, Pallas kernels, body(): pl.pallas_call(functools.partial(kernel, count, windows, 1.0 / math.sqrt(...  64.4 us
    unnamed x1, local copies, waits for them, and re-layouts  2.26 us

profile of v2, /device:TPU:16, one launch (start us, length us, event | category | flops | bytes accessed | tf_op | source)
XLA Modules:
  0.0 66.7 jit_solution(16316642714526982323)
XLA Ops:
  0.0 64.4 %shard_map.37 = f32[512,512]{1,0:T(8,128)} custom-call(bf16[128,2,4,16,128]{4,3,2,1,0:T(8,128)(2,1)} %bitcast.10, s32[2,512]{1,0:T(2,128)} %bitcast.12, s32[1,512]{1,0:T(1,128)} %bitcast.13), custom_call_target="tpu_custom_call" | custom-call | tf_op jit(solution)/shard_map/pallas_call | solution.py:337
  64.4 2.3 %copy.6 = f32[4,128,512]{2,1,0:T(8,128)} copy(f32[4,128,512]{2,1,0:T(8,128)} %bitcast.11) | data formatting | bytes 2097152

commit v3 on v2

--- a/solution.py
+++ b/solution.py
@@ -15,19 +15,20 @@
 PIECES = 4
 WHITEN_ROWS = 64
 UNROLL = 16
+RETURNS = 2
 MESH = pl.DeviceIdType.MESH
 
 
-def kernel(count, windows, norm_factor, own_hbm, pairs_ref, live_ref, out_ref,
-           own, beside, across, white, spread, planes, lag, acc, base, turn,
+def kernel(count, windows, norm_factor, own_hbm, pairs_ref, live_ref, out_hbm, back_in,
+           own, shared, beside, across, white, spread, planes, lag, acc, base, turn,
            sums, handed, red, heard, common,
-           far_pairs, far_live, tab_v, tab_a0, tab_b0, tab_a1, tab_b1, back_out, back_in,
+           far_pairs, far_live, tab_v, tab_a0, tab_b0, tab_a1, tab_b1, back_out,
            load_sem, beside_send, beside_recv, across_send, across_recv, sum_send, sum_recv,
-           tab_send, tab_recv, back_send, back_recv, smem_sem):
+           tab_send, tab_recv, back_send, back_recv, smem_sem, out_sem):
     slabs, rows = own.shape[:2]
     span = windows * 16
     bins = slabs * SLAB
-    pairs = out_ref.shape[0]
+    pairs = out_hbm.shape[0]
     me = lax.axis_index("row")
     core = lax.rem(me, 2)
     partner = me + 1 - 2 * core
@@ -49,7 +50,7 @@
         return pltpu.make_async_copy(own_hbm.at[:, :, q], own.at[q], load_sem.at[q])
 
     def send_beside(q):
-        return remote(own_hbm.at[:, :, q], beside.at[q], beside_send.at[q], beside_recv.at[q], partner)
+        return remote(shared.at[q], beside.at[q], beside_send.at[q], beside_recv.at[q], partner)
 
     def send_across(q, k, target):
         at = pl.ds(pl.multiple_of(k * piece, piece), piece)
@@ -59,8 +60,9 @@
         return (remote(pairs_ref, far_pairs, tab_send.at[0], tab_recv.at[0], target),
                 remote(live_ref, far_live, tab_send.at[1], tab_recv.at[1], target))
 
-    def send_back(target):
-        return remote(back_out, back_in, back_send.at[0], back_recv.at[0], target)
+    def send_back(t, target):
+        at = pl.ds(t * (pairs // RETURNS), pairs // RETURNS)
+        return remote(back_out.at[at], back_in.at[at], back_send.at[t], back_recv.at[t], target)
 
     for q in range(slabs):
         load(q).start()
@@ -87,11 +89,9 @@
             for k in range(PIECES):
                 send_across(q, k, left).start()
 
-    for q in range(slabs):
-        send_beside(q).start()
-
     acc[...] = jnp.zeros_like(acc)
-    white[pl.ds(zero_row, 8)] = jnp.zeros((8,) + white.shape[1:], jnp.float32)
+    for h in range(2):
+        white[h, pl.ds(zero_row, 8)] = jnp.zeros((8,) + white.shape[2:], jnp.float32)
 
     for q in range(slabs):
         load(q).wait()
@@ -213,7 +213,7 @@
     size = WHITEN_ROWS
     depth = windows * 8
 
-    def whiten(q, source, i, start):
+    def whiten(q, source, i, start, keep):
         at = pl.ds(pl.multiple_of(i * size, size), size)
         spread[...] = source[q, at].astype(jnp.float32).reshape(size * span, LANES)
         re = spread[pl.ds(0, size * depth, stride=2), :].reshape(size, depth, LANES) - common[0, q][None]
@@ -226,70 +226,103 @@
         level += jnp.dot(lo, same, preferred_element_type=jnp.float32)
         scale = (1.0 / (level * (1.0 / BAND) + 1e-06)).reshape(size, depth, LANES)
         to = pl.ds(pl.multiple_of(start + i * size, 8), size)
-        wr = (re * scale).astype(jnp.bfloat16).astype(jnp.float32)
-        wi = (im * scale).astype(jnp.bfloat16).astype(jnp.float32)
-        white[to, 0:windows] = wr.reshape(size, windows, 8, LANES)
-        white[to, windows : 2 * windows] = wi.reshape(size, windows, 8, LANES)
-
-    def whiten_all(q, source, start):
+        for r, part in enumerate((re, im)):
+            rounded = (part * scale).astype(jnp.bfloat16)
+            if keep:
+                shared[q, at, r] = rounded
+            wide = rounded.astype(jnp.float32).reshape(size, windows, 8, LANES)
+            white[lax.rem(q, 2), to, r * windows : (r + 1) * windows] = wide
+
+    def whiten_own(q):
         @pl.loop(0, rows // size)
         def _(i):
-            whiten(q, source, i, start)
-
-    def correlate(group, q):
+            whiten(q, own, i, 0, True)
+
+        send_beside(q).start()
+
+    def expand(q):
+        @pl.loop(0, rows // 16)
+        def _(i):
+            at = pl.ds(pl.multiple_of(i * 16, 16), 16)
+            to = pl.ds(pl.multiple_of(rows + i * 16, 16), 16)
+            wide = beside[q, at].astype(jnp.float32)
+            white[lax.rem(q, 2), to] = wide.reshape(16, 2 * windows, 8, LANES)
+
+    def correlate(group, q, tile, after=None):
         table_a, table_b = tables[2 * group], tables[2 * group + 1]
-
-        @pl.loop(0, pairs // UNROLL)
-        def _(i):
-            at = pl.multiple_of(i * UNROLL * 8, 64)
-            for u in range(UNROLL):
-                p = i * UNROLL + u
-                a, b = white.at[table_a[0, p]], white.at[table_b[0, p]]
-                cross_re, cross_im = None, None
-                for w in range(windows):
-                    ar, ai, br, bi = a[w], a[windows + w], b[w], b[windows + w]
-                    part_re, part_im = ar * br + ai * bi, ai * br - ar * bi
-                    cross_re = part_re if cross_re is None else cross_re + part_re
-                    cross_im = part_im if cross_im is None else cross_im + part_im
-                to = pl.ds(at + (u // 8) * 64 + u % 8, 8, stride=8)
-                planes[0, to, :] = cross_re
-                planes[1, to, :] = cross_im
-
-        total = None
-        for r in range(2):
-            plane = planes[r].reshape(pairs // 8, 8, 8, LANES)
-            cross = jnp.concatenate([plane[:, f].reshape(pairs, LANES).astype(jnp.bfloat16) for f in range(8)], axis=1)
-            part = jnp.dot(cross, lag[q, r], preferred_element_type=jnp.float32)
-            total = part if total is None else total + part
-        acc[group] += total
+        source = white.at[lax.rem(q, 2)]
+        for t in range(pairs // tile):
+            @pl.loop(0, tile // UNROLL)
+            def _(i, t=t):
+                at = pl.multiple_of(i * UNROLL * 8, 64)
+                for u in range(UNROLL):
+                    p = t * tile + i * UNROLL + u
+                    a, b = source.at[table_a[0, p]], source.at[table_b[0, p]]
+                    cross_re, cross_im = None, None
+                    for w in range(windows):
+                        ar, ai, br, bi = a[w], a[windows + w], b[w], b[windows + w]
+                        part_re, part_im = ar * br + ai * bi, ai * br - ar * bi
+                        cross_re = part_re if cross_re is None else cross_re + part_re
+                        cross_im = part_im if cross_im is None else cross_im + part_im
+                    to = pl.ds(at + (u // 8) * 64 + u % 8, 8, stride=8)
+                    planes[0, to, :] = cross_re
+                    planes[1, to, :] = cross_im
+
+            total = None
+            for r in range(2):
+                plane = planes[r, 0 : tile * 8].reshape(tile // 8, 8, 8, LANES)
+                cross = [plane[:, f].reshape(tile, LANES).astype(jnp.bfloat16) for f in range(8)]
+                part = jnp.dot(jnp.concatenate(cross, axis=1), lag[q, r], preferred_element_type=jnp.float32)
+                total = part if total is None else total + part
+            if after is None:
+                acc[group, t * tile : (t + 1) * tile] += total
+            else:
+                after(t, acc[group, t * tile : (t + 1) * tile] + total)
+
+    def give_back(t, total):
+        tile = pairs // RETURNS
+        back_out[t * tile : (t + 1) * tile] = total.astype(jnp.bfloat16)
+        send_back(t, right).start()
+
+    whiten_own(0)
 
     @pl.loop(0, slabs)
     def _(q):
-        whiten_all(q, own, 0)
+        @pl.when(q < slabs - 1)
+        def _():
+            whiten_own(q + 1)
+
         send_beside(q).wait_recv()
-        whiten_all(q, beside, rows)
+        expand(q)
 
         @pl.when(gets)
         def _():
-            for k in range(PIECES):
-                send_across(q, k, right).wait_recv()
-            whiten_all(q, across, 2 * rows)
-            correlate(1, q)
+            @pl.loop(0, rows // size)
+            def _(i):
+                for k in range(size // piece):
+                    send_across(q, i * (size // piece) + k, right).wait_recv()
+                whiten(q, across, i, 2 * rows, False)
+
+            @pl.when(q < slabs - 1)
+            def _():
+                correlate(1, q, pairs)
 
             @pl.when(q == slabs - 1)
             def _():
-                back_out[...] = acc[1].astype(jnp.bfloat16)
-                send_back(right).start()
-
-        correlate(0, q)
+                correlate(1, q, pairs // RETURNS, give_back)
+
+        correlate(0, q, pairs)
+
+    acc[0] = acc[0] * norm_factor
+    store = pltpu.make_async_copy(acc.at[0], out_hbm, out_sem.at[0])
+    store.start()
 
     @pl.when(gives)
     def _():
-        send_back(left).wait_recv()
-        acc[0] += back_in[...].astype(jnp.float32)
-
-    out_ref[...] = acc[0] * norm_factor
-
+        for t in range(RETURNS):
+            send_back(t, left).wait_recv()
+
+    store.wait()
     for q in range(slabs):
         send_beside(q).wait_send()
 
@@ -315,7 +348,8 @@
 
     @pl.when(gets)
     def _():
-        send_back(right).wait_send()
+        for t in range(RETURNS):
+            send_back(t, right).wait_send()
 
 
 def body(spectra, pair_channels, pair_live):
@@ -334,14 +368,18 @@
     dma = pltpu.SemaphoreType.DMA
     f32, bf16, i32 = jnp.float32, jnp.bfloat16, jnp.int32
     raw = pltpu.VMEM((slabs, rows, windows, 16, LANES), bf16)
-    result = pl.pallas_call(
-        functools.partial(kernel, count, windows, 1.0 / math.sqrt(bins * windows)),
-        out_shape=jax.ShapeDtypeStruct((pairs, LAGS), f32),
+    norm_factor = 1.0 / math.sqrt(bins * windows)
+    result, back = pl.pallas_call(
+        functools.partial(kernel, count, windows, norm_factor),
+        out_shape=[jax.ShapeDtypeStruct((pairs, LAGS), f32), jax.ShapeDtypeStruct((pairs, LAGS), bf16)],
         in_specs=[pl.BlockSpec(memory_space=pl.ANY), vmem, vmem],
-        out_specs=vmem,
+        out_specs=[pl.BlockSpec(memory_space=pl.ANY)] * 2,
         scratch_shapes=[
-            raw, raw, raw,
-            pltpu.VMEM((3 * rows + 8, 2 * windows, 8, LANES), f32),
+            raw,
+            pltpu.VMEM((slabs, rows, 2, windows * 8, LANES), bf16),
+            pltpu.VMEM((slabs, rows, 2, windows * 8, LANES), bf16),
+            raw,
+            pltpu.VMEM((2, 3 * rows + 8, 2 * windows, 8, LANES), f32),
             pltpu.VMEM((WHITEN_ROWS * span, LANES), f32),
             pltpu.VMEM((2, pairs * 8, LANES), f32),
             pltpu.VMEM((slabs, 2, SLAB, LAGS), bf16),
@@ -359,13 +397,15 @@
             pltpu.SMEM((1, pairs), i32), pltpu.SMEM((1, pairs), i32),
             pltpu.SMEM((1, pairs), i32), pltpu.SMEM((1, pairs), i32),
             pltpu.VMEM((pairs, LAGS), bf16),
-            pltpu.VMEM((pairs, LAGS), bf16),
             dma((slabs,)), dma((slabs,)), dma((slabs,)), dma((slabs, PIECES)), dma((slabs, PIECES)),
-            dma((rounds + 1,)), dma((rounds + 1,)), dma((2,)), dma((2,)), dma((1,)), dma((1,)), dma((4,)),
+            dma((rounds + 1,)), dma((rounds + 1,)), dma((2,)), dma((2,)), dma((RETURNS,)), dma((RETURNS,)), dma((4,)), dma((1,)),
         ],
         compiler_params=pltpu.CompilerParams(
             collective_id=0, has_side_effects=True, vmem_limit_bytes=60 * 2**20),
     )(view, index, live)
+    me = lax.axis_index("row")
+    gives = (me & 1) < jnp.minimum(me, 1)
+    result = result + jnp.where(gives, back.astype(f32) * norm_factor, 0.0)
     return result.reshape(tile_count, tile_pairs, LAGS)
 
 

time: 66.8 us -> 64.2 us (0.961)
  Pallas kernels: 64.4 us -> 61.5 us
  other arithmetic: 0 us -> 2.51 us
  local copies, waits for them, and re-layouts: 2.26 us -> 0 us
    pallas_call x1, Pallas kernels: 64.4 us -> 61.5 us  [body(): pl.pallas_call(functools.partial(kernel, count, windows, norm_factor), ou...]
    add x0 -> x1, other arithmetic: none -> 2.51 us  [body(): result = result + jnp.where(gives, back.astype(f32) * norm_factor, 0.0)]
    unnamed x1 -> x0, local copies, waits for them, and re-layouts: 2.26 us -> none
where the time goes in v3:
time: 64.2 us; the launch traced here: 64 us
  Pallas kernels  61.5 us (96%)
  other arithmetic  2.51 us (4%)
    pallas_call x1, Pallas kernels, body(): pl.pallas_call(functools.partial(kernel, count, windows, norm_factor), ou...  61.5 us
    add x1, other arithmetic, body(): result = result + jnp.where(gives, back.astype(f32) * norm_factor, 0.0)  2.51 us

profile of v3, /device:TPU:16, one launch (start us, length us, event | category | flops | bytes accessed | tf_op | source)
XLA Modules:
  0.0 64.0 jit_solution(10266005415487446273)
XLA Ops:
  0.0 61.5 %shard_map.37 = (f32[512,512]{1,0:T(8,128)}, bf16[512,512]{1,0:T(8,128)(2,1)}) custom-call(bf16[128,2,4,16,128]{4,3,2,1,0:T(8,128)(2,1)} %bitcast.10, s32[2,512]{1,0:T(2,128)} %bitcast.11, s32[1,512]{1,0:T(1,128)} %bitcast.12), custom_call_target="tpu_custom_call" | custom-call | tf_op jit(solution)/shard_map/pallas_call | solution.py:372
  61.5 2.5 %select_add_fusion = f32[512,512]{1,0:T(8,128)} fusion(f32[512,512]{1,0:T(8,128)} %get-tuple-element.7, bf16[512,512]{1,0:T(8,128)(2,1)} %get-tuple-element.8, pred[]{:T(512)S(6)} %lt.3), kind=kLoop, calls=%fused_computation | loop fusion | flops 1048576 | bytes 2621441 | tf_op jit(solution)/shard_map/add | solution.py:408

commit v4 on v3

--- a/solution.py
+++ b/solution.py
@@ -19,12 +19,12 @@
 MESH = pl.DeviceIdType.MESH
 
 
-def kernel(count, windows, norm_factor, own_hbm, pairs_ref, live_ref, out_hbm, back_in,
+def kernel(count, windows, norm_factor, own_hbm, pairs_hbm, live_hbm, out_hbm, back_in,
            own, shared, beside, across, white, spread, planes, lag, acc, base, turn,
            sums, handed, red, heard, common,
-           far_pairs, far_live, tab_v, tab_a0, tab_b0, tab_a1, tab_b1, back_out,
+           near_pairs, near_live, far_pairs, far_live, tab_v, tab_a0, tab_b0, tab_a1, tab_b1, back_out,
            load_sem, beside_send, beside_recv, across_send, across_recv, sum_send, sum_recv,
-           tab_send, tab_recv, back_send, back_recv, smem_sem, out_sem):
+           tab_load, tab_send, tab_recv, back_send, back_recv, smem_sem, out_sem):
     slabs, rows = own.shape[:2]
     span = windows * 16
     bins = slabs * SLAB
@@ -57,8 +57,11 @@
         return remote(own_hbm.at[at, :, q], across.at[q, at], across_send.at[q, k], across_recv.at[q, k], target)
 
     def send_tables(target):
-        return (remote(pairs_ref, far_pairs, tab_send.at[0], tab_recv.at[0], target),
-                remote(live_ref, far_live, tab_send.at[1], tab_recv.at[1], target))
+        return (remote(pairs_hbm, far_pairs, tab_send.at[0], tab_recv.at[0], target),
+                remote(live_hbm, far_live, tab_send.at[1], tab_recv.at[1], target))
+
+    fetches = (pltpu.make_async_copy(pairs_hbm, near_pairs, tab_load.at[0]),
+               pltpu.make_async_copy(live_hbm, near_live, tab_load.at[1]))
 
     def send_back(t, target):
         at = pl.ds(t * (pairs // RETURNS), pairs // RETURNS)
@@ -66,6 +69,8 @@
 
     for q in range(slabs):
         load(q).start()
+    for fetch in fetches:
+        fetch.start()
 
     barrier = pltpu.get_barrier_semaphore()
     hops = [me ^ (1 << r) for r in range(1, rounds)]
@@ -167,7 +172,9 @@
             slot = jnp.where((offset >= 0) & (offset < rows), offset + start, slot)
         return slot
 
-    first, second, live = pairs_ref[0:1], pairs_ref[1:2], live_ref[...]
+    for fetch in fetches:
+        fetch.wait()
+    first, second, live = near_pairs[0:1], near_pairs[1:2], near_live[...]
     far_device = jnp.where(gets, me + 1, -2)
     regions = ((me, 0), (partner, rows), (far_device, 2 * rows))
     tab_v[0] = jnp.where(live > 0, place(first, regions), zero_row)
@@ -210,12 +217,11 @@
     lane_r = lax.broadcasted_iota(jnp.int32, (LANES, LANES), 0) // BAND
     lane_c = lax.broadcasted_iota(jnp.int32, (LANES, LANES), 1) // BAND
     same = (lane_r == lane_c).astype(jnp.float32).astype(jnp.bfloat16)
-    size = WHITEN_ROWS
     depth = windows * 8
 
-    def whiten(q, source, i, start, keep):
+    def whiten(q, source, i, size, start, keep):
         at = pl.ds(pl.multiple_of(i * size, size), size)
-        spread[...] = source[q, at].astype(jnp.float32).reshape(size * span, LANES)
+        spread[0 : size * span] = source[q, at].astype(jnp.float32).reshape(size * span, LANES)
         re = spread[pl.ds(0, size * depth, stride=2), :].reshape(size, depth, LANES) - common[0, q][None]
         im = spread[pl.ds(1, size * depth, stride=2), :].reshape(size, depth, LANES) - common[1, q][None]
         power = (re * re + im * im).reshape(size * depth, LANES)
@@ -234,9 +240,9 @@
             white[lax.rem(q, 2), to, r * windows : (r + 1) * windows] = wide
 
     def whiten_own(q):
-        @pl.loop(0, rows // size)
+        @pl.loop(0, rows // WHITEN_ROWS)
         def _(i):
-            whiten(q, own, i, 0, True)
+            whiten(q, own, i, WHITEN_ROWS, 0, True)
 
         send_beside(q).start()
 
@@ -297,11 +303,10 @@
 
         @pl.when(gets)
         def _():
-            @pl.loop(0, rows // size)
-            def _(i):
-                for k in range(size // piece):
-                    send_across(q, i * (size // piece) + k, right).wait_recv()
-                whiten(q, across, i, 2 * rows, False)
+            @pl.loop(0, PIECES)
+            def _(k):
+                send_across(q, k, right).wait_recv()
+                whiten(q, across, k, piece, 2 * rows, False)
 
             @pl.when(q < slabs - 1)
             def _():
@@ -364,7 +369,6 @@
     live = pair_live.reshape(1, pairs)
     rounds = count.bit_length() - 1
     span = windows * 16
-    vmem = pl.BlockSpec(memory_space=pltpu.VMEM)
     dma = pltpu.SemaphoreType.DMA
     f32, bf16, i32 = jnp.float32, jnp.bfloat16, jnp.int32
     raw = pltpu.VMEM((slabs, rows, windows, 16, LANES), bf16)
@@ -372,7 +376,7 @@
     result, back = pl.pallas_call(
         functools.partial(kernel, count, windows, norm_factor),
         out_shape=[jax.ShapeDtypeStruct((pairs, LAGS), f32), jax.ShapeDtypeStruct((pairs, LAGS), bf16)],
-        in_specs=[pl.BlockSpec(memory_space=pl.ANY), vmem, vmem],
+        in_specs=[pl.BlockSpec(memory_space=pltpu.HBM)] * 3,
         out_specs=[pl.BlockSpec(memory_space=pl.ANY)] * 2,
         scratch_shapes=[
             raw,
@@ -393,16 +397,18 @@
             pltpu.VMEM((2, slabs, windows * 8, LANES), f32),
             pltpu.VMEM((2, pairs), i32),
             pltpu.VMEM((1, pairs), i32),
+            pltpu.VMEM((2, pairs), i32),
+            pltpu.VMEM((1, pairs), i32),
             pltpu.VMEM((4, 1, pairs), i32),
             pltpu.SMEM((1, pairs), i32), pltpu.SMEM((1, pairs), i32),
             pltpu.SMEM((1, pairs), i32), pltpu.SMEM((1, pairs), i32),
             pltpu.VMEM((pairs, LAGS), bf16),
             dma((slabs,)), dma((slabs,)), dma((slabs,)), dma((slabs, PIECES)), dma((slabs, PIECES)),
-            dma((rounds + 1,)), dma((rounds + 1,)), dma((2,)), dma((2,)), dma((RETURNS,)), dma((RETURNS,)), dma((4,)), dma((1,)),
+            dma((rounds + 1,)), dma((rounds + 1,)), dma((2,)), dma((2,)), dma((2,)), dma((RETURNS,)), dma((RETURNS,)), dma((4,)), dma((1,)),
         ],
         compiler_params=pltpu.CompilerParams(
-            collective_id=0, has_side_effects=True, vmem_limit_bytes=60 * 2**20),
-    )(view, index, live)
+            collective_id=0, has_side_effects=True, vmem_limit_bytes=50 * 2**20),
+    )(view, *(pltpu.with_memory_space_constraint(table, pltpu.HBM) for table in (index, live)))
     me = lax.axis_index("row")
     gives = (me & 1) < jnp.minimum(me, 1)
     result = result + jnp.where(gives, back.astype(f32) * norm_factor, 0.0)

time: 64.2 us -> 61.9 us (0.964)
  other arithmetic: 2.51 us -> 1.16 us
  Pallas kernels: 61.5 us -> 60.6 us
    add x1, other arithmetic: 2.51 us -> 1.16 us  [body(): result = result + jnp.where(gives, back.astype(f32) * norm_factor, 0.0)]
    pallas_call x1, Pallas kernels: 61.5 us -> 60.6 us  [body(): pl.pallas_call(functools.partial(kernel, count, windows, norm_factor), ou...]
where the time goes in v4:
time: 61.9 us; the launch traced here: 61.8 us
  Pallas kernels  60.6 us (98%)
  other arithmetic  1.16 us (2%)
    pallas_call x1, Pallas kernels, body(): pl.pallas_call(functools.partial(kernel, count, windows, norm_factor), ou...  60.6 us

profile of v4, /device:TPU:16, one launch (start us, length us, event | category | flops | bytes accessed | tf_op | source)
XLA Modules:
  0.0 61.8 jit_solution(5636166174537971393)
XLA Ops:
  0.0 60.6 %shard_map.37 = (f32[512,512]{1,0:T(8,128)S(1)}, bf16[512,512]{1,0:T(8,128)(2,1)S(1)}) custom-call(bf16[128,2,4,16,128]{4,3,2,1,0:T(8,128)(2,1)} %bitcast.10, s32[2,512]{1,0:T(2,128)} %bitcast.11, s32[1,512]{1,0:T(1,128)} %bitcast.12), custom_call_target="tpu_custom_call" | custom-call | tf_op jit(solution)/shard_map/pallas_call | solution.py:376
  60.6 1.2 %select_add_fusion = f32[512,512]{1,0:T(8,128)} fusion(f32[512,512]{1,0:T(8,128)S(1)} %get-tuple-element.7, bf16[512,512]{1,0:T(8,128)(2,1)S(1)} %get-tuple-element.8, pred[]{:T(512)S(6)} %lt.3), kind=kLoop, calls=%fused_computation | loop fusion | flops 1048576 | bytes 2621441 | tf_op jit(solution)/shard_map/add | solution.py:414

commit v5 on v4

--- a/solution.py
+++ b/solution.py
@@ -12,7 +12,8 @@
 LAGS = 512
 LANES = 128
 SLAB = 8 * LANES
-PIECES = 4
+PIECES = 2
+LAST_PIECES = 2
 WHITEN_ROWS = 64
 UNROLL = 16
 RETURNS = 2
@@ -20,10 +21,10 @@
 
 
 def kernel(count, windows, norm_factor, own_hbm, pairs_hbm, live_hbm, out_hbm, back_in,
-           own, shared, beside, across, white, spread, planes, lag, acc, base, turn,
+           own, shared, beside, across, across_last, white, spread, planes, lag, acc, base, turn,
            sums, handed, red, heard, common,
            near_pairs, near_live, far_pairs, far_live, tab_v, tab_a0, tab_b0, tab_a1, tab_b1, back_out,
-           load_sem, beside_send, beside_recv, across_send, across_recv, sum_send, sum_recv,
+           load_sem, beside_send, beside_recv, across_send, across_recv, last_send, last_recv, sum_send, sum_recv,
            tab_load, tab_send, tab_recv, back_send, back_recv, smem_sem, out_sem):
     slabs, rows = own.shape[:2]
     span = windows * 16
@@ -33,6 +34,7 @@
     core = lax.rem(me, 2)
     partner = me + 1 - 2 * core
     rounds = count.bit_length() - 1
+    last = slabs - 1
     channels = count * rows
     piece = rows // PIECES
     gets = (core == 1) & (me < count - 1)
@@ -56,6 +58,12 @@
         at = pl.ds(pl.multiple_of(k * piece, piece), piece)
         return remote(own_hbm.at[at, :, q], across.at[q, at], across_send.at[q, k], across_recv.at[q, k], target)
 
+    def send_last(w, k, target):
+        size = rows // LAST_PIECES
+        at = pl.ds(k * size, size)
+        return remote(shared.at[last, w, at], across_last.at[w, at],
+                      last_send.at[w, k], last_recv.at[w, k], target)
+
     def send_tables(target):
         return (remote(pairs_hbm, far_pairs, tab_send.at[0], tab_recv.at[0], target),
                 remote(live_hbm, far_live, tab_send.at[1], tab_recv.at[1], target))
@@ -89,7 +97,7 @@
         for copy in send_tables(left):
             copy.start()
 
-        @pl.loop(0, slabs)
+        @pl.loop(0, last)
         def _(q):
             for k in range(PIECES):
                 send_across(q, k, left).start()
@@ -235,7 +243,8 @@
         for r, part in enumerate((re, im)):
             rounded = (part * scale).astype(jnp.bfloat16)
             if keep:
-                shared[q, at, r] = rounded
+                for w in range(windows):
+                    shared[q, w, at, r] = rounded[:, w * 8 : (w + 1) * 8]
             wide = rounded.astype(jnp.float32).reshape(size, windows, 8, LANES)
             white[lax.rem(q, 2), to, r * windows : (r + 1) * windows] = wide
 
@@ -251,10 +260,19 @@
         def _(i):
             at = pl.ds(pl.multiple_of(i * 16, 16), 16)
             to = pl.ds(pl.multiple_of(rows + i * 16, 16), 16)
-            wide = beside[q, at].astype(jnp.float32)
-            white[lax.rem(q, 2), to] = wide.reshape(16, 2 * windows, 8, LANES)
-
-    def correlate(group, q, tile, after=None):
+            for w in range(windows):
+                wide = beside[q, w, at].astype(jnp.float32)
+                white[lax.rem(q, 2), to, w] = wide[:, 0]
+                white[lax.rem(q, 2), to, windows + w] = wide[:, 1]
+
+    def expand_last(w, k):
+        size = rows // LAST_PIECES
+        wide = across_last[w, k * size : (k + 1) * size].astype(jnp.float32)
+        to = slice(2 * rows + k * size, 2 * rows + (k + 1) * size)
+        white[last % 2, to, w] = wide[:, 0]
+        white[last % 2, to, windows + w] = wide[:, 1]
+
+    def correlate(group, q, tile, after=None, used=tuple(range(windows))):
         table_a, table_b = tables[2 * group], tables[2 * group + 1]
         source = white.at[lax.rem(q, 2)]
         for t in range(pairs // tile):
@@ -265,7 +283,7 @@
                     p = t * tile + i * UNROLL + u
                     a, b = source.at[table_a[0, p]], source.at[table_b[0, p]]
                     cross_re, cross_im = None, None
-                    for w in range(windows):
+                    for w in used:
                         ar, ai, br, bi = a[w], a[windows + w], b[w], b[windows + w]
                         part_re, part_im = ar * br + ai * bi, ai * br - ar * bi
                         cross_re = part_re if cross_re is None else cross_re + part_re
@@ -298,23 +316,36 @@
         def _():
             whiten_own(q + 1)
 
+        @pl.when(gives & (q == last - 1))
+        def _():
+            for w in range(windows):
+                for k in range(LAST_PIECES):
+                    send_last(w, k, left).start()
+
         send_beside(q).wait_recv()
         expand(q)
 
         @pl.when(gets)
         def _():
-            @pl.loop(0, PIECES)
-            def _(k):
-                send_across(q, k, right).wait_recv()
-                whiten(q, across, k, piece, 2 * rows, False)
-
-            @pl.when(q < slabs - 1)
+            @pl.when(q < last)
             def _():
+                @pl.loop(0, PIECES)
+                def _(k):
+                    send_across(q, k, right).wait_recv()
+                    whiten(q, across, k, piece, 2 * rows, False)
+
                 correlate(1, q, pairs)
 
-            @pl.when(q == slabs - 1)
+            @pl.when(q == last)
             def _():
-                correlate(1, q, pairs // RETURNS, give_back)
+                for w in range(windows):
+                    for k in range(LAST_PIECES):
+                        send_last(w, k, right).wait_recv()
+                        expand_last(w, k)
+                    if w < windows - 1:
+                        correlate(1, q, pairs, None, (w,))
+                    else:
+                        correlate(1, q, pairs // RETURNS, give_back, (w,))
 
         correlate(0, q, pairs)
 
@@ -346,10 +377,13 @@
         for copy in send_tables(left):
             copy.wait_send()
 
-        @pl.loop(0, slabs)
+        @pl.loop(0, last)
         def _(q):
             for k in range(PIECES):
                 send_across(q, k, left).wait_send()
+        for w in range(windows):
+            for k in range(LAST_PIECES):
+                send_last(w, k, left).wait_send()
 
     @pl.when(gets)
     def _():
@@ -380,9 +414,10 @@
         out_specs=[pl.BlockSpec(memory_space=pl.ANY)] * 2,
         scratch_shapes=[
             raw,
-            pltpu.VMEM((slabs, rows, 2, windows * 8, LANES), bf16),
-            pltpu.VMEM((slabs, rows, 2, windows * 8, LANES), bf16),
-            raw,
+            pltpu.VMEM((slabs, windows, rows, 2, 8, LANES), bf16),
+            pltpu.VMEM((slabs, windows, rows, 2, 8, LANES), bf16),
+            pltpu.VMEM((slabs - 1, rows, windows, 16, LANES), bf16),
+            pltpu.VMEM((windows, rows, 2, 8, LANES), bf16),
             pltpu.VMEM((2, 3 * rows + 8, 2 * windows, 8, LANES), f32),
             pltpu.VMEM((WHITEN_ROWS * span, LANES), f32),
             pltpu.VMEM((2, pairs * 8, LANES), f32),
@@ -403,7 +438,8 @@
             pltpu.SMEM((1, pairs), i32), pltpu.SMEM((1, pairs), i32),
             pltpu.SMEM((1, pairs), i32), pltpu.SMEM((1, pairs), i32),
             pltpu.VMEM((pairs, LAGS), bf16),
-            dma((slabs,)), dma((slabs,)), dma((slabs,)), dma((slabs, PIECES)), dma((slabs, PIECES)),
+            dma((slabs,)), dma((slabs,)), dma((slabs,)), dma((slabs - 1, PIECES)), dma((slabs - 1, PIECES)),
+            dma((windows, LAST_PIECES)), dma((windows, LAST_PIECES)),
             dma((rounds + 1,)), dma((rounds + 1,)), dma((2,)), dma((2,)), dma((2,)), dma((RETURNS,)), dma((RETURNS,)), dma((4,)), dma((1,)),
         ],
         compiler_params=pltpu.CompilerParams(

time: 61.9 us -> 61.6 us (level)
  no operation moved by 1% of the time
where the time goes in v5:
time: 61.6 us; the launch traced here: 61.4 us
  Pallas kernels  60.3 us (98%)
  other arithmetic  1.16 us (2%)
    pallas_call x1, Pallas kernels, body(): pl.pallas_call(functools.partial(kernel, count, windows, norm_factor), ou...  60.3 us

profile of v5, /device:TPU:16, one launch (start us, length us, event | category | flops | bytes accessed | tf_op | source)
XLA Modules:
  0.0 61.4 jit_solution(1801302237403165017)
XLA Ops:
  0.0 60.3 %shard_map.37 = (f32[512,512]{1,0:T(8,128)S(1)}, bf16[512,512]{1,0:T(8,128)(2,1)S(1)}) custom-call(bf16[128,2,4,16,128]{4,3,2,1,0:T(8,128)(2,1)} %bitcast.10, s32[2,512]{1,0:T(2,128)} %bitcast.11, s32[1,512]{1,0:T(1,128)} %bitcast.12), custom_call_target="tpu_custom_call" | custom-call | tf_op jit(solution)/shard_map/pallas_call | solution.py:410
  60.3 1.2 %select_add_fusion = f32[512,512]{1,0:T(8,128)} fusion(f32[512,512]{1,0:T(8,128)S(1)} %get-tuple-element.7, bf16[512,512]{1,0:T(8,128)(2,1)S(1)} %get-tuple-element.8, pred[]{:T(512)S(6)} %lt.3), kind=kLoop, calls=%fused_computation | loop fusion | flops 1048576 | bytes 2621441 | tf_op jit(solution)/shard_map/add | solution.py:450

commit v6 on v5

--- a/solution.py
+++ b/solution.py
@@ -15,21 +15,21 @@
 PIECES = 2
 LAST_PIECES = 2
 WHITEN_ROWS = 64
-UNROLL = 16
+UNROLL = 32
 RETURNS = 2
 MESH = pl.DeviceIdType.MESH
 
 
-def kernel(count, windows, norm_factor, own_hbm, pairs_hbm, live_hbm, out_hbm, back_in,
+def kernel(count, windows, norm_factor, own_hbm, pairs_hbm, live_hbm, out_ref,
            own, shared, beside, across, across_last, white, spread, planes, lag, acc, base, turn,
            sums, handed, red, heard, common,
-           near_pairs, near_live, far_pairs, far_live, tab_v, tab_a0, tab_b0, tab_a1, tab_b1, back_out,
+           near_pairs, near_live, far_pairs, far_live, tab_v, tab_a0, tab_b0, tab_a1, tab_b1, back,
            load_sem, beside_send, beside_recv, across_send, across_recv, last_send, last_recv, sum_send, sum_recv,
-           tab_load, tab_send, tab_recv, back_send, back_recv, smem_sem, out_sem):
+           tab_load, tab_send, tab_recv, back_send, back_recv, smem_sem):
     slabs, rows = own.shape[:2]
     span = windows * 16
     bins = slabs * SLAB
-    pairs = out_hbm.shape[0]
+    pairs = out_ref.shape[0]
     me = lax.axis_index("row")
     core = lax.rem(me, 2)
     partner = me + 1 - 2 * core
@@ -73,7 +73,7 @@
 
     def send_back(t, target):
         at = pl.ds(t * (pairs // RETURNS), pairs // RETURNS)
-        return remote(back_out.at[at], back_in.at[at], back_send.at[t], back_recv.at[t], target)
+        return remote(back.at[at], back.at[at], back_send.at[t], back_recv.at[t], target)
 
     for q in range(slabs):
         load(q).start()
@@ -305,7 +305,7 @@
 
     def give_back(t, total):
         tile = pairs // RETURNS
-        back_out[t * tile : (t + 1) * tile] = total.astype(jnp.bfloat16)
+        back[t * tile : (t + 1) * tile] = total.astype(jnp.bfloat16)
         send_back(t, right).start()
 
     whiten_own(0)
@@ -349,16 +349,15 @@
 
         correlate(0, q, pairs)
 
-    acc[0] = acc[0] * norm_factor
-    store = pltpu.make_async_copy(acc.at[0], out_hbm, out_sem.at[0])
-    store.start()
+    out_ref[...] = acc[0] * norm_factor
 
     @pl.when(gives)
     def _():
         for t in range(RETURNS):
             send_back(t, left).wait_recv()
-
-    store.wait()
+            at = pl.ds(t * (pairs // RETURNS), pairs // RETURNS)
+            out_ref[at] = out_ref[at] + back[at].astype(jnp.float32) * norm_factor
+
     for q in range(slabs):
         send_beside(q).wait_send()
 
@@ -407,11 +406,11 @@
     f32, bf16, i32 = jnp.float32, jnp.bfloat16, jnp.int32
     raw = pltpu.VMEM((slabs, rows, windows, 16, LANES), bf16)
     norm_factor = 1.0 / math.sqrt(bins * windows)
-    result, back = pl.pallas_call(
+    result = pl.pallas_call(
         functools.partial(kernel, count, windows, norm_factor),
-        out_shape=[jax.ShapeDtypeStruct((pairs, LAGS), f32), jax.ShapeDtypeStruct((pairs, LAGS), bf16)],
+        out_shape=jax.ShapeDtypeStruct((pairs, LAGS), f32),
         in_specs=[pl.BlockSpec(memory_space=pltpu.HBM)] * 3,
-        out_specs=[pl.BlockSpec(memory_space=pl.ANY)] * 2,
+        out_specs=pl.BlockSpec(memory_space=pltpu.VMEM),
         scratch_shapes=[
             raw,
             pltpu.VMEM((slabs, windows, rows, 2, 8, LANES), bf16),
@@ -440,14 +439,11 @@
             pltpu.VMEM((pairs, LAGS), bf16),
             dma((slabs,)), dma((slabs,)), dma((slabs,)), dma((slabs - 1, PIECES)), dma((slabs - 1, PIECES)),
             dma((windows, LAST_PIECES)), dma((windows, LAST_PIECES)),
-            dma((rounds + 1,)), dma((rounds + 1,)), dma((2,)), dma((2,)), dma((2,)), dma((RETURNS,)), dma((RETURNS,)), dma((4,)), dma((1,)),
+            dma((rounds + 1,)), dma((rounds + 1,)), dma((2,)), dma((2,)), dma((2,)), dma((RETURNS,)), dma((RETURNS,)), dma((4,)),
         ],
         compiler_params=pltpu.CompilerParams(
             collective_id=0, has_side_effects=True, vmem_limit_bytes=50 * 2**20),
     )(view, *(pltpu.with_memory_space_constraint(table, pltpu.HBM) for table in (index, live)))
-    me = lax.axis_index("row")
-    gives = (me & 1) < jnp.minimum(me, 1)
-    result = result + jnp.where(gives, back.astype(f32) * norm_factor, 0.0)
     return result.reshape(tile_count, tile_pairs, LAGS)
 
 

time: 61.6 us -> 61.4 us (level)
  other arithmetic: 1.16 us -> 0 us
  local copies, waits for them, and re-layouts: 0 us -> 0.97 us
    add x1 -> x0, other arithmetic: 1.16 us -> none  [body(): result = result + jnp.where(gives, back.astype(f32) * norm_factor, 0.0)]
    unnamed x0 -> x1, local copies, waits for them, and re-layouts: none -> 0.97 us
where the time goes in v6:
time: 61.4 us; the launch traced here: 61.2 us
  Pallas kernels  60.3 us (98%)
  local copies, waits for them, and re-layouts  0.97 us (2%)
    pallas_call x1, Pallas kernels, body(): pl.pallas_call(functools.partial(kernel, count, windows, norm_factor), ou...  60.3 us

profile of v6, /device:TPU:16, one launch (start us, length us, event | category | flops | bytes accessed | tf_op | source)
XLA Modules:
  0.0 61.2 jit_solution(13217171638178089270)
XLA Ops:
  0.0 60.3 %shard_map.37 = f32[512,512]{1,0:T(8,128)S(1)} custom-call(bf16[128,2,4,16,128]{4,3,2,1,0:T(8,128)(2,1)} %bitcast.11, s32[2,512]{1,0:T(2,128)} %bitcast.12, s32[1,512]{1,0:T(1,128)} %bitcast.13), custom_call_target="tpu_custom_call" | custom-call | tf_op jit(solution)/shard_map/pallas_call | solution.py:409
  60.3 1.0 %copy.6 = f32[4,128,512]{2,1,0:T(8,128)} copy(f32[4,128,512]{2,1,0:T(8,128)S(1)} %bitcast.10) | data formatting | bytes 2097152

commit v7 on v6

--- a/solution.py
+++ b/solution.py
@@ -12,8 +12,8 @@
 LAGS = 512
 LANES = 128
 SLAB = 8 * LANES
-PIECES = 2
-LAST_PIECES = 2
+PIECES = 1
+LAST_PIECES = 1
 WHITEN_ROWS = 64
 UNROLL = 32
 RETURNS = 2
@@ -332,7 +332,8 @@
                 @pl.loop(0, PIECES)
                 def _(k):
                     send_across(q, k, right).wait_recv()
-                    whiten(q, across, k, piece, 2 * rows, False)
+                    whiten(q, across, 2 * k, piece // 2, 2 * rows, False)
+                    whiten(q, across, 2 * k + 1, piece // 2, 2 * rows, False)
 
                 correlate(1, q, pairs)
 

time: 61.4 us -> 61.4 us (level)
  no operation moved by 1% of the time
where the time goes in v7:
time: 61.4 us; the launch traced here: 61.2 us
  Pallas kernels  60.2 us (98%)
  local copies, waits for them, and re-layouts  0.97 us (2%)
    pallas_call x1, Pallas kernels, body(): pl.pallas_call(functools.partial(kernel, count, windows, norm_factor), ou...  60.2 us

profile of v7, /device:TPU:16, one launch (start us, length us, event | category | flops | bytes accessed | tf_op | source)
XLA Modules:
  0.0 61.2 jit_solution(10044554417738237916)
XLA Ops:
  0.0 60.2 %shard_map.37 = f32[512,512]{1,0:T(8,128)S(1)} custom-call(bf16[128,2,4,16,128]{4,3,2,1,0:T(8,128)(2,1)} %bitcast.11, s32[2,512]{1,0:T(2,128)} %bitcast.12, s32[1,512]{1,0:T(1,128)} %bitcast.13), custom_call_target="tpu_custom_call" | custom-call | tf_op jit(solution)/shard_map/pallas_call | solution.py:410
  60.2 1.0 %copy.6 = f32[4,128,512]{2,1,0:T(8,128)} copy(f32[4,128,512]{2,1,0:T(8,128)S(1)} %bitcast.10) | data formatting | bytes 2097152

commit v8 on v6

--- a/solution.py
+++ b/solution.py
@@ -75,21 +75,20 @@
         at = pl.ds(t * (pairs // RETURNS), pairs // RETURNS)
         return remote(back.at[at], back.at[at], back_send.at[t], back_recv.at[t], target)
 
+    barrier = pltpu.get_barrier_semaphore()
+    hops = [me ^ (1 << r) for r in range(1, rounds)]
+    for p in (partner, near):
+        pl.semaphore_signal(barrier, inc=1, device_id={"row": p}, device_id_type=MESH)
+
+    @pl.when(core == 1)
+    def _():
+        for p in hops:
+            pl.semaphore_signal(barrier, inc=1, device_id={"row": p}, device_id_type=MESH)
+
     for q in range(slabs):
         load(q).start()
     for fetch in fetches:
         fetch.start()
-
-    barrier = pltpu.get_barrier_semaphore()
-    hops = [me ^ (1 << r) for r in range(1, rounds)]
-    for p in (partner, near):
-        pl.semaphore_signal(barrier, inc=1, device_id={"row": p}, device_id_type=MESH)
-
-    @pl.when(core == 1)
-    def _():
-        for p in hops:
-            pl.semaphore_signal(barrier, inc=1, device_id={"row": p}, device_id_type=MESH)
-
     pl.semaphore_wait(barrier, 2 + core * len(hops))
 
     @pl.when(gives)

time: 61.4 us -> 61.4 us (level)
  no operation moved by 1% of the time
where the time goes in v8:
time: 61.4 us; the launch traced here: 61.2 us
  Pallas kernels  60.3 us (98%)
  local copies, waits for them, and re-layouts  0.97 us (2%)
    pallas_call x1, Pallas kernels, body(): pl.pallas_call(functools.partial(kernel, count, windows, norm_factor), ou...  60.3 us

profile of v8, /device:TPU:16, one launch (start us, length us, event | category | flops | bytes accessed | tf_op | source)
XLA Modules:
  0.0 61.2 jit_solution(11090548000500202015)
XLA Ops:
  0.0 60.3 %shard_map.37 = f32[512,512]{1,0:T(8,128)S(1)} custom-call(bf16[128,2,4,16,128]{4,3,2,1,0:T(8,128)(2,1)} %bitcast.11, s32[2,512]{1,0:T(2,128)} %bitcast.12, s32[1,512]{1,0:T(1,128)} %bitcast.13), custom_call_target="tpu_custom_call" | custom-call | tf_op jit(solution)/shard_map/pallas_call | solution.py:408
  60.3 1.0 %copy.6 = f32[4,128,512]{2,1,0:T(8,128)} copy(f32[4,128,512]{2,1,0:T(8,128)S(1)} %bitcast.10) | data formatting | bytes 2097152
